TPU v7x, 32 devices: a whole 2x2x4 slice. The times are simulated.
32 devices in a mesh: row: 4 (over y, x), col: 4 (over z), depth: 2 (over core).
Axes of the slice: x: 2, y: 2, z: 4, core: 2. Of those that a mesh axis runs over, the one named last changes fastest.
Arguments:
- matrix_panel: bfloat16 [12288, 65536], P('row', 'col'), may hold values from -0.1484375 to 0.1484375
- start_block: bfloat16 [12288, 64], P('row', 'depth'), may hold values from -6 to 6
- stored_basis: float32 [12288, 1024], P('row'), may hold values from -2.2 to 2.2
Outputs:
- new_block: float32 [12288, 64], P('row', 'depth')
- coefficients: float32 [1024, 64], P(None, 'depth')
- triangle: float32 [64, 64], replicated
All inputs are finite; a program needn't handle non-finite values.
Results may differ from a plain program's by a relative error of at most 0.0023.
Values may be sent and summed in bfloat16 or wider, within the bound.
A program may use at most 256 MiB of HBM per device.

v0:
```python
import jax
import jax.numpy as jnp
from jax import lax
from jax.sharding import PartitionSpec as P

HIGHEST = lax.Precision.HIGHEST


def contract_rows(left_side, right_side, mode):
    return lax.dot_general(
        left_side,
        right_side,
        (((0,), (0,)), ((), ())),
        precision=mode,
        preferred_element_type=jnp.float32,
    )


def factor_gram(gram_matrix):
    lower_factor = jnp.linalg.cholesky(gram_matrix)
    identity = jnp.eye(gram_matrix.shape[0], dtype=jnp.float32)
    inverse = jax.scipy.linalg.solve_triangular(lower_factor, identity, lower=True)
    return (lower_factor, inverse)


def orthonormal_pass(stored_basis, block_cols, reduce_sum, row_total):
    projection = reduce_sum(contract_rows(stored_basis, block_cols, HIGHEST)) / row_total
    remainder = block_cols - jnp.dot(
        stored_basis, projection, precision=HIGHEST, preferred_element_type=jnp.float32
    )
    gram_matrix = reduce_sum(contract_rows(remainder, remainder, HIGHEST)) / row_total
    lower_factor, inverse = factor_gram(gram_matrix)
    normed = jnp.dot(remainder, inverse.T, precision=HIGHEST, preferred_element_type=jnp.float32)
    return (projection, lower_factor, normed)


def per_device(matrix_panel, start_block, stored_basis):
    row_total = stored_basis.shape[0] * lax.axis_size("row")
    half_cols = start_block.shape[1]
    depth_index = lax.axis_index("depth")
    whole_start = lax.all_gather(start_block, "depth", axis=1, tiled=True)
    half_rows = matrix_panel.shape[0] // 2
    panel_rows = lax.dynamic_slice_in_dim(matrix_panel, depth_index * half_rows, half_rows, 0)
    start_rows = lax.dynamic_slice_in_dim(whole_start, depth_index * half_rows, half_rows, 0)
    basis_rows = lax.dynamic_slice_in_dim(stored_basis, depth_index * half_rows, half_rows, 0)
    mixed_cols = lax.psum(contract_rows(panel_rows, start_rows, None), ("row", "depth")).astype(
        jnp.bfloat16
    )
    image_block = lax.psum(
        jnp.dot(panel_rows, mixed_cols, preferred_element_type=jnp.float32), "col"
    )

    def sum_layers(value):
        return lax.psum(value, ("row", "depth"))

    proj_first, lower_first, normed_first = orthonormal_pass(
        basis_rows, image_block, sum_layers, row_total
    )
    proj_second, lower_second, normed_second = orthonormal_pass(
        basis_rows, normed_first, sum_layers, row_total
    )
    new_block = lax.all_to_all(normed_second, "depth", split_axis=1, concat_axis=0, tiled=True)
    coef_whole = proj_first + jnp.dot(
        proj_second, lower_first.T, precision=HIGHEST, preferred_element_type=jnp.float32
    )
    coefficients = lax.dynamic_slice_in_dim(coef_whole, depth_index * half_cols, half_cols, 1)
    triangle = jnp.dot(
        lower_second.T, lower_first.T, precision=HIGHEST, preferred_element_type=jnp.float32
    )
    return (new_block, coefficients, triangle)


def solution(mesh):
    placed = (P("row", "col"), P("row", "depth"), P("row", None))
    return jax.shard_map(
        per_device,
        mesh=mesh,
        in_specs=placed,
        out_specs=(P("row", "depth"), P(None, "depth"), P()),
        check_vma=False,
    )
```

profile of v0, /device:TPU:0, one launch (start us, length us, event | category | flops | bytes accessed | tf_op | source)
XLA Modules:
  0.0 405.6 jit_solution(3928022254567349980)
XLA Ops:
  7.2 0.0 all-reduce.5.cloned.1.call-start
  7.2 2.4 all_gather.3
  9.6 20.5 %fusion.2 = f32[16384,64]{0,1:T(8,128)} fusion(bf16[3072,16384]{1,0:T(8,128)(2,1)} %param.6, s32[]{:T(128)S(6)} %select_n.11, bf16[3072,64]{0,1:T(8,128)(2,1)S(1)} %all_gather.3), kind=kOutput, calls=%fused_computation.2 | convolution fusion | flops 3221225472 | bytes 54723584 | tf_op jit(solution)/shard_map/dot_general | solution.py:10
  30.1 89.5 %all-reduce.10 = bf16[16384,64]{0,1:T(8,128)(2,1)S(1)} all-reduce(f32[16384,64]{0,1:T(8,128)} %fusion.2), channel_id=1, replica_groups=mesh['row'=4,'col'=4,'depth'=2] {'row','depth'}, use_global_device_ids=true, to_apply=%region_0.0 | all-reduce | flops 1048576 | bytes 6291456 | tf_op jit(solution)/shard_map/psum | solution.py:46
  119.6 22.6 %fusion = f32[1536,64]{0,1:T(8,128)} fusion(bf16[3072,16384]{1,0:T(8,128)(2,1)} %param.6, s32[]{:T(128)S(6)} %select_n.11, bf16[16384,64]{0,1:T(8,128)(2,1)S(1)} %all-reduce.10), kind=kOutput, calls=%fused_computation | convolution fusion | flops 3221225472 | bytes 52822020 | tf_op jit(solution)/shard_map/dot_general | solution.py:50
  142.2 0.0 all-reduce.5.cloned.1.call-update
  142.2 0.0 all-reduce.7.cloned.1.call-start
  142.3 36.9 %all-reduce.5.cloned.1.call-done = f32[1536,64]{0,1:T(8,128)} async-done(((f32[1536,64]{0,1:T(8,128)}), f32[1536,64]{0,1:T(8,128)}) %all-reduce.5.cloned.1.call-update) | async-done | bytes 393232 | tf_op jit(solution)/shard_map/psum | solution.py:49
  179.2 7.6 %fusion.10 = f32[1024,64]{0,1:T(8,128)} fusion(f32[1536,64]{0,1:T(8,128)} %all-reduce.5.cloned.1.call-done, f32[3072,1024]{1,0:T(8,128)} %param.8, s32[]{:T(128)S(6)} %select_n.11), kind=kOutput, calls=%fused_computation.10 | convolution fusion | flops 1207959552 | bytes 6946820 | tf_op jit(solution)/shard_map/dot_general | solution.py:10
  186.8 0.0 all-reduce.7.cloned.1.call-update
  186.8 0.2 all-reduce.9.cloned.1.call-start
  187.0 53.1 %all-reduce.7.cloned.1.call-done = f32[1024,64]{0,1:T(8,128)} async-done(((f32[1024,64]{0,1:T(8,128)}), f32[1024,64]{0,1:T(8,128)}) %all-reduce.7.cloned.1.call-update) | async-done | bytes 262160 | tf_op jit(solution)/shard_map/psum | solution.py:54
  240.1 0.0 copy-start
  240.1 9.1 %fusion.12 = f32[1536,64]{0,1:T(8,128)S(1)} fusion(f32[1536,64]{0,1:T(8,128)} %all-reduce.5.cloned.1.call-done, f32[3072,1024]{1,0:T(8,128)} %param.8, s32[]{:T(128)S(6)} %select_n.11, f32[1024,64]{0,1:T(8,128)} %all-reduce.7.cloned.1.call-done), kind=kOutput, calls=%fused_computation.12 | convolution fusion | flops 1208123392 | bytes 7340036 | tf_op jit(solution)/shard_map/dot_general | solution.py:28
  249.2 0.5 fusion.56
  249.6 22.4 %psum.45 = f32[64,64]{0,1:T(8,128)S(1)} all-reduce(f32[64,64]{0,1:T(8,128)S(1)} %fusion.56), channel_id=1, replica_groups=mesh['row'=4,'col'=4,'depth'=2] {'row','depth'}, use_global_device_ids=true, to_apply=%region_3.0 | all-reduce | flops 4096 | bytes 32768 | tf_op jit(solution)/shard_map/psum | solution.py:54
  272.0 0.1 copy.12
  272.1 5.8 %cholesky.44 = f32[64,64]{1,0:T(8,128)S(1)} custom-call(f32[64,64]{1,0:T(8,128)S(1)} %fusion.32), custom_call_target="Cholesky" | custom-call | tf_op jit(solution)/shard_map/jit(cholesky)/cholesky | solution.py:20
  278.0 0.6 compare_reduce_fusion.1
  278.6 0.7 select_bitcast_fusion.1
  279.3 4.9 %custom-call.6 = f32[1,64,64]{1,2,0:T(8,128)S(1)} custom-call(f32[1,64,64]{2,1,0:T(8,128)S(1)} %select_bitcast_fusion.1), custom_call_target="InvertDiagBlocksLowerTriangular" | custom-call | tf_op jit(solution)/shard_map/jit(_solve_triangular)/triangular_solve | solution.py:22
  284.2 0.3 fusion.27
  284.4 0.5 fusion.57
  284.9 7.6 %fusion.6 = f32[1024,64]{0,1:T(8,128)} fusion(f32[1536,64]{0,1:T(8,128)S(1)} %fusion.57, f32[3072,1024]{1,0:T(8,128)} %param.8, s32[]{:T(128)S(6)} %select_n.11), kind=kOutput, calls=%fused_computation.6 | convolution fusion | flops 1207959552 | bytes 6946820 | tf_op jit(solution)/shard_map/dot_general | solution.py:10
  292.5 0.0 all-reduce.9.cloned.1.call-update
  292.5 0.0 copy-done
  292.5 53.0 %all-reduce.9.cloned.1.call-done = f32[1024,64]{0,1:T(8,128)} async-done(((f32[1024,64]{0,1:T(8,128)}), f32[1024,64]{0,1:T(8,128)}) %all-reduce.9.cloned.1.call-update) | async-done | bytes 262160 | tf_op jit(solution)/shard_map/psum | solution.py:54
  345.5 8.1 %fusion.15 = f32[1536,64]{0,1:T(8,128)S(1)} fusion(f32[1536,64]{0,1:T(8,128)S(1)} %fusion.57, f32[3072,1024]{1,0:T(8,128)} %param.8, s32[]{:T(128)S(6)} %select_n.11, f32[1024,64]{0,1:T(8,128)} %all-reduce.9.cloned.1.call-done), kind=kOutput, calls=%fused_computation.13 | convolution fusion | flops 1208123392 | bytes 7340036 | tf_op jit(solution)/shard_map/dot_general | solution.py:28
  353.7 0.5 fusion.58
  354.1 22.4 %psum.47 = f32[64,64]{0,1:T(8,128)S(1)} all-reduce(f32[64,64]{0,1:T(8,128)S(1)} %fusion.58), channel_id=1, replica_groups=mesh['row'=4,'col'=4,'depth'=2] {'row','depth'}, use_global_device_ids=true, to_apply=%region_7.10 | all-reduce | flops 4096 | bytes 32768 | tf_op jit(solution)/shard_map/psum | solution.py:54
  376.5 0.1 copy.14
  376.6 5.8 %cholesky.55 = f32[64,64]{1,0:T(8,128)S(1)} custom-call(f32[64,64]{1,0:T(8,128)S(1)} %fusion.30), custom_call_target="Cholesky" | custom-call | tf_op jit(solution)/shard_map/jit(cholesky)/cholesky | solution.py:20
  382.5 0.6 compare_reduce_fusion
  383.1 2.1 fusion.34
  385.3 0.7 select_bitcast_fusion
  385.9 4.9 %custom-call.7 = f32[1,64,64]{1,2,0:T(8,128)S(1)} custom-call(f32[1,64,64]{2,1,0:T(8,128)S(1)} %select_bitcast_fusion), custom_call_target="InvertDiagBlocksLowerTriangular" | custom-call | tf_op jit(solution)/shard_map/jit(_solve_triangular)/triangular_solve | solution.py:22
  390.8 0.3 fusion.25
  391.1 0.5 fusion.59
  391.6 4.0 all_to_all.19
  395.6 0.8 copy.18
  396.4 2.0 fusion.19
  398.4 0.7 dynamic-slice_add_fusion
  (7 shorter events, 0.1 us)
Async XLA Ops:
  7.2 172.0 %all-reduce.5.cloned.1.call-start = ((), (), s32[]{:S(2)}) async-start(), calls=%async_computation.1 | async-start | bytes 786432 | tf_op jit(solution)/shard_map/psum | solution.py:49
  142.2 97.8 %all-reduce.7.cloned.1.call-start = ((), (), s32[]{:S(2)}) async-start(), calls=%async_computation.2 | async-start | bytes 524288 | tf_op jit(solution)/shard_map/psum | solution.py:54
  186.8 158.8 %all-reduce.9.cloned.1.call-start = ((), (), s32[]{:S(2)}) async-start(), calls=%async_computation.3 | async-start | bytes 524288 | tf_op jit(solution)/shard_map/psum | solution.py:54
  240.1 52.4 %copy-start = (f32[1024,64]{0,1:T(8,128)S(1)}, f32[1024,64]{0,1:T(8,128)}, u32[]{:S(2)}) copy-start(f32[1024,64]{0,1:T(8,128)} %all-reduce.7.cloned.1.call-done) | copy-start | bytes 786436
Sparse Core Ops, SparseCore 0:
  142.3 36.8 all-reduce.4
  186.9 53.1 all-reduce.6
  292.6 52.8 all-reduce.8
where the time goes:
time: 406 us
  waiting for transfers between devices  143 us (35%)
  blocking collectives  141 us (35%)
  matrix products  82 us (20%)
  other arithmetic  24.9 us (6%)
  between operations  13.9 us (3%)
    psum x2, waiting for transfers between devices, sum_layers(): return lax.psum(value, ('row', 'depth'))  106 us
    psum x1, blocking collectives, per_device(): lax.psum(contract_rows(panel_rows, start_rows, None), ('row', 'depth'))  89.5 us
    psum x2, blocking collectives, sum_layers(): return lax.psum(value, ('row', 'depth'))  44.7 us
    psum x1, waiting for transfers between devices, per_device(): lax.psum(jnp.dot(panel_rows, mixed_cols, preferred_element_type=jnp.float...  36.9 us
    dot_general x5, matrix products, contract_rows(): lax.dot_general(left_side, right_side, (((0,), (0,)), ((), ())), precisio...  36.5 us
    dot_general x1, matrix products, per_device(): jnp.dot(panel_rows, mixed_cols, preferred_element_type=jnp.float32)  22.6 us
    dot_general x2, matrix products, orthonormal_pass(): jnp.dot(stored_basis, projection, precision=HIGHEST, preferred_element_ty...  17.2 us
    another operation x6, other arithmetic, factor_gram(): lower_factor = jnp.linalg.cholesky(gram_matrix)  13 us
  transfers between devices with their start and end apart: 3, of which 3 were waited for; matrix products, arithmetic and copies ran while one was open for 0% of the time, Pallas kernels for 0%

commit v1 on v0

--- a/solution.py
+++ b/solution.py
@@ -43,9 +43,9 @@
     panel_rows = lax.dynamic_slice_in_dim(matrix_panel, depth_index * half_rows, half_rows, 0)
     start_rows = lax.dynamic_slice_in_dim(whole_start, depth_index * half_rows, half_rows, 0)
     basis_rows = lax.dynamic_slice_in_dim(stored_basis, depth_index * half_rows, half_rows, 0)
-    mixed_cols = lax.psum(contract_rows(panel_rows, start_rows, None), ("row", "depth")).astype(
-        jnp.bfloat16
-    )
+    mixed_cols = jnp.sum(
+        lax.all_gather(contract_rows(panel_rows, start_rows, None), ("row", "depth")), axis=0
+    ).astype(jnp.bfloat16)
     image_block = lax.psum(
         jnp.dot(panel_rows, mixed_cols, preferred_element_type=jnp.float32), "col"
     )

time: 406 us -> 521 us (1.28)
  waiting for transfers between devices: 143 us -> 307 us
  blocking collectives: 141 us -> 51.4 us
  local copies, waits for them, and re-layouts: 0.93 us -> 29.1 us
  other arithmetic: 24.9 us -> 36.9 us
    all_gather x0 -> x1, waiting for transfers between devices: none -> 164 us  [per_device(): lax.all_gather(contract_rows(panel_rows, start_rows, None), ('row', 'dept...]
    psum x1 -> x0, blocking collectives: 89.5 us -> none  [per_device(): lax.psum(contract_rows(panel_rows, start_rows, None), ('row', 'depth'))]
    unnamed x2 -> x3, local copies, waits for them, and re-layouts: 0.01 us -> 28.2 us
    reduce_sum x0 -> x1, other arithmetic: none -> 12 us  [per_device(): jnp.sum(lax.all_gather(contract_rows(panel_rows, start_rows, None), ('row...]
  transfers between devices with their start and end apart: 3 -> 4, of which waited for: 3 -> 4; matrix products, arithmetic and copies ran while one was open for 0% -> 0% of each run, Pallas kernels for 0% -> 0%
where the time goes in v1:
time: 521 us
  waiting for transfers between devices  307 us (59%)
  matrix products  82.7 us (16%)
  blocking collectives  51.4 us (10%)
  other arithmetic  36.9 us (7%)
  local copies, waits for them, and re-layouts  29.1 us (6%)
  between operations  13.9 us (3%)
    all_gather x1, waiting for transfers between devices, per_device(): lax.all_gather(contract_rows(panel_rows, start_rows, None), ('row', 'dept...  164 us
    psum x2, waiting for transfers between devices, sum_layers(): return lax.psum(value, ('row', 'depth'))  106 us
    psum x2, blocking collectives, sum_layers(): return lax.psum(value, ('row', 'depth'))  44.9 us
    psum x1, waiting for transfers between devices, per_device(): lax.psum(jnp.dot(panel_rows, mixed_cols, preferred_element_type=jnp.float...  37 us
    dot_general x5, matrix products, contract_rows(): lax.dot_general(left_side, right_side, (((0,), (0,)), ((), ())), precisio...  36.7 us
    unnamed x3, local copies, waits for them, and re-layouts  28.2 us
    dot_general x1, matrix products, per_device(): jnp.dot(panel_rows, mixed_cols, preferred_element_type=jnp.float32)  23.2 us
    dot_general x2, matrix products, orthonormal_pass(): jnp.dot(stored_basis, projection, precision=HIGHEST, preferred_element_ty...  17.2 us
  transfers between devices with their start and end apart: 4, of which 4 were waited for; matrix products, arithmetic and copies ran while one was open for 0% of the time, Pallas kernels for 0%

profile of v1, /device:TPU:0, one launch (start us, length us, event | category | flops | bytes accessed | tf_op | source)
XLA Modules:
  0.0 521.1 jit_solution(12249975972337129338)
XLA Ops:
  7.2 0.0 all-gather.3.cloned.1.call-start
  7.2 2.4 all_gather.9
  9.6 20.6 %fusion.2 = f32[16384,64]{0,1:T(8,128)} fusion(bf16[3072,16384]{1,0:T(8,128)(2,1)} %param.6, s32[]{:T(128)S(6)} %select_n.11, bf16[3072,64]{0,1:T(8,128)(2,1)S(1)} %all_gather.9), kind=kOutput, calls=%fused_computation.2 | convolution fusion | flops 3221225472 | bytes 54723584 | tf_op jit(solution)/shard_map/dot_general | solution.py:10
  30.2 0.0 all-gather.3.cloned.1.call-update
  30.3 0.0 all-reduce.4.cloned.1.call-start
  30.3 163.5 %all-gather.3.cloned.1.call-done = f32[131072,64]{0,1:T(8,128)} async-done(((f32[16384,64]{0,1:T(8,128)}), f32[131072,64]{0,1:T(8,128)}) %all-gather.3.cloned.1.call-update) | async-done | bytes 33554448 | tf_op jit(solution)/shard_map/all_gather | solution.py:47
  193.8 28.2 %copy.19 = f32[8,8,8,16384]{3,2,1,0:T(8,128)S(1)} copy(f32[8,8,8,16384]{3,1,2,0:T(8,128)} %bitcast.38) | data formatting | bytes 67108864
  222.0 12.0 %bitcast_reduce_fusion = bf16[16384,64]{0,1:T(8,128)(2,1)} fusion(f32[8,8,8,16384]{3,2,1,0:T(8,128)S(1)} %copy.19), kind=kLoop, calls=%fused_computation.4 | loop fusion | flops 7340032 | bytes 35651584 | tf_op jit(solution)/shard_map/reduce_sum | solution.py:46
  234.0 23.2 %fusion = f32[1536,64]{0,1:T(8,128)} fusion(bf16[3072,16384]{1,0:T(8,128)(2,1)} %param.6, s32[]{:T(128)S(6)} %select_n.11, bf16[16384,64]{0,1:T(8,128)(2,1)} %bitcast_reduce_fusion), kind=kOutput, calls=%fused_computation | convolution fusion | flops 3221225472 | bytes 52822020 | tf_op jit(solution)/shard_map/dot_general | solution.py:50
  257.2 0.0 all-reduce.4.cloned.1.call-update
  257.3 0.2 all-reduce.6.cloned.1.call-start
  257.5 37.0 %all-reduce.4.cloned.1.call-done = f32[1536,64]{0,1:T(8,128)} async-done(((f32[1536,64]{0,1:T(8,128)}), f32[1536,64]{0,1:T(8,128)}) %all-reduce.4.cloned.1.call-update) | async-done | bytes 393232 | tf_op jit(solution)/shard_map/psum | solution.py:49
  294.5 7.6 %fusion.10 = f32[1024,64]{0,1:T(8,128)} fusion(f32[1536,64]{0,1:T(8,128)} %all-reduce.4.cloned.1.call-done, f32[3072,1024]{1,0:T(8,128)} %param.8, s32[]{:T(128)S(6)} %select_n.11), kind=kOutput, calls=%fused_computation.11 | convolution fusion | flops 1207959552 | bytes 6946820 | tf_op jit(solution)/shard_map/dot_general | solution.py:10
  302.1 0.0 all-reduce.6.cloned.1.call-update
  302.1 0.0 all-reduce.8.cloned.1.call-start
  302.1 53.2 %all-reduce.6.cloned.1.call-done = f32[1024,64]{0,1:T(8,128)} async-done(((f32[1024,64]{0,1:T(8,128)}), f32[1024,64]{0,1:T(8,128)}) %all-reduce.6.cloned.1.call-update) | async-done | bytes 262160 | tf_op jit(solution)/shard_map/psum | solution.py:54
  355.4 0.0 copy-start
  355.4 9.1 %fusion.12 = f32[1536,64]{0,1:T(8,128)S(1)} fusion(f32[1536,64]{0,1:T(8,128)} %all-reduce.4.cloned.1.call-done, f32[3072,1024]{1,0:T(8,128)} %param.8, s32[]{:T(128)S(6)} %select_n.11, f32[1024,64]{0,1:T(8,128)} %all-reduce.6.cloned.1.call-done), kind=kOutput, calls=%fused_computation.13 | convolution fusion | flops 1208123392 | bytes 7340036 | tf_op jit(solution)/shard_map/dot_general | solution.py:28
  364.5 0.5 fusion.56
  364.9 22.6 %psum.37 = f32[64,64]{0,1:T(8,128)S(1)} all-reduce(f32[64,64]{0,1:T(8,128)S(1)} %fusion.56), channel_id=1, replica_groups=mesh['row'=4,'col'=4,'depth'=2] {'row','depth'}, use_global_device_ids=true, to_apply=%region_3.0 | all-reduce | flops 4096 | bytes 32768 | tf_op jit(solution)/shard_map/psum | solution.py:54
  387.5 0.1 copy.12
  387.6 5.8 %cholesky.44 = f32[64,64]{1,0:T(8,128)S(1)} custom-call(f32[64,64]{1,0:T(8,128)S(1)} %fusion.32), custom_call_target="Cholesky" | custom-call | tf_op jit(solution)/shard_map/jit(cholesky)/cholesky | solution.py:20
  393.5 0.6 compare_reduce_fusion.1
  394.1 0.7 select_bitcast_fusion.1
  394.8 4.9 custom-call.6
  399.7 0.3 fusion.27
  400.0 0.5 fusion.57
  400.4 7.6 %fusion.6 = f32[1024,64]{0,1:T(8,128)} fusion(f32[1536,64]{0,1:T(8,128)S(1)} %fusion.57, f32[3072,1024]{1,0:T(8,128)} %param.8, s32[]{:T(128)S(6)} %select_n.11), kind=kOutput, calls=%fused_computation.7 | convolution fusion | flops 1207959552 | bytes 6946820 | tf_op jit(solution)/shard_map/dot_general | solution.py:10
  408.0 0.0 all-reduce.8.cloned.1.call-update
  408.0 0.0 copy-done
  408.1 53.0 %all-reduce.8.cloned.1.call-done = f32[1024,64]{0,1:T(8,128)} async-done(((f32[1024,64]{0,1:T(8,128)}), f32[1024,64]{0,1:T(8,128)}) %all-reduce.8.cloned.1.call-update) | async-done | bytes 262160 | tf_op jit(solution)/shard_map/psum | solution.py:54
  461.1 8.1 %fusion.15 = f32[1536,64]{0,1:T(8,128)S(1)} fusion(f32[1536,64]{0,1:T(8,128)S(1)} %fusion.57, f32[3072,1024]{1,0:T(8,128)} %param.8, s32[]{:T(128)S(6)} %select_n.11, f32[1024,64]{0,1:T(8,128)} %all-reduce.8.cloned.1.call-done), kind=kOutput, calls=%fused_computation.14 | convolution fusion | flops 1208123392 | bytes 7340036 | tf_op jit(solution)/shard_map/dot_general | solution.py:28
  469.2 0.5 fusion.58
  469.7 22.4 %psum.39 = f32[64,64]{0,1:T(8,128)S(1)} all-reduce(f32[64,64]{0,1:T(8,128)S(1)} %fusion.58), channel_id=1, replica_groups=mesh['row'=4,'col'=4,'depth'=2] {'row','depth'}, use_global_device_ids=true, to_apply=%region_7.10 | all-reduce | flops 4096 | bytes 32768 | tf_op jit(solution)/shard_map/psum | solution.py:54
  492.0 0.1 copy.14
  492.1 5.8 %cholesky.55 = f32[64,64]{1,0:T(8,128)S(1)} custom-call(f32[64,64]{1,0:T(8,128)S(1)} %fusion.30), custom_call_target="Cholesky" | custom-call | tf_op jit(solution)/shard_map/jit(cholesky)/cholesky | solution.py:20
  498.0 0.6 compare_reduce_fusion
  498.6 2.1 fusion.34
  500.8 0.7 select_bitcast_fusion
  501.4 4.9 custom-call.7
  506.3 0.3 fusion.25
  506.6 0.5 fusion.59
  507.1 4.0 all_to_all.19
  511.1 0.8 copy.18
  511.9 2.0 fusion.19
  513.9 0.7 dynamic-slice_add_fusion
  (7 shorter events, 0.1 us)
Async XLA Ops:
  7.2 186.7 %all-gather.3.cloned.1.call-start = ((), (), s32[]{:S(2)}) async-start(), calls=%async_computation.4 | async-start | bytes 37748736 | tf_op jit(solution)/shard_map/all_gather | solution.py:47
  30.3 264.2 %all-reduce.4.cloned.1.call-start = ((), (), s32[]{:S(2)}) async-start(), calls=%async_computation.1 | async-start | bytes 786432 | tf_op jit(solution)/shard_map/psum | solution.py:49
  257.3 98.1 %all-reduce.6.cloned.1.call-start = ((), (), s32[]{:S(2)}) async-start(), calls=%async_computation.2 | async-start | bytes 524288 | tf_op jit(solution)/shard_map/psum | solution.py:54
  302.1 159.0 %all-reduce.8.cloned.1.call-start = ((), (), s32[]{:S(2)}) async-start(), calls=%async_computation.3 | async-start | bytes 524288 | tf_op jit(solution)/shard_map/psum | solution.py:54
  355.4 52.7 %copy-start = (f32[1024,64]{0,1:T(8,128)S(1)}, f32[1024,64]{0,1:T(8,128)}, u32[]{:S(2)}) copy-start(f32[1024,64]{0,1:T(8,128)} %all-reduce.6.cloned.1.call-done) | copy-start | bytes 786436
Sparse Core Ops, SparseCore 0:
  30.4 163.4 all-gather.2
  257.4 37.0 all-reduce.3
  302.2 53.1 all-reduce.5
  408.1 52.8 all-reduce.7
